TPU v7x, 32 devices: a whole 2x2x4 slice. The times are simulated.
32 devices in a mesh: expert: 16 (over z, y, x), tok: 2 (over core).
Axes of the slice: x: 2, y: 2, z: 4, core: 2. Of those that a mesh axis runs over, the one named last changes fastest.
Arguments:
- tokens: bfloat16 [2048, 3584], P(('expert', 'tok')), may hold values from -6 to 6
- routes: int32 [2048, 8], P(('expert', 'tok')), may hold values from 0 to 15, all different within a row; in each aligned block of 64 rows (0 to 63, 64 to 127, ...) at most 36 rows name the same one
- gates: float32 [2048, 8], P(('expert', 'tok')), may hold values from 0.05 to 1
- upstream: bfloat16 [2048, 3584], P(('expert', 'tok')), may hold values from -6 to 6
- w_up: bfloat16 [16, 3584, 1024], P('expert', None, 'tok'), may hold values from -0.09375 to 0.09375
- w_down: bfloat16 [16, 1024, 3584], P('expert', 'tok'), may hold values from -0.1875 to 0.1875
Outputs:
- mixed: bfloat16 [2048, 3584], P(('expert', 'tok'))
- d_tokens: bfloat16 [2048, 3584], P(('expert', 'tok'))
- d_gates: float32 [2048, 8], P(('expert', 'tok'))
- grad_up: bfloat16 [16, 3584, 1024], P('expert', None, 'tok')
- grad_down: bfloat16 [16, 1024, 3584], P('expert', 'tok')
Inputs may be any that keep to these rules, and one draw needn't show every extreme that they name: `routes`: each token names 8 different experts. At most 36 of the 64 tokens of one device name the same expert, and in every draw the tokens of some device name some expert exactly 36 times.
All inputs are finite; a program needn't handle non-finite values.
Results may differ from a plain program's by a relative error of at most 0.0065.
Values may be sent and summed in bfloat16 or wider, within the bound.
A program may use at most 192 MiB of HBM per device.

v0:
```python
import jax
import jax.numpy as jnp
from jax import lax
from jax.sharding import PartitionSpec as P

GELU_C = 0.7978845608028654
GELU_A = 0.044715


def gelu_value(hidden):
    inner_arg = GELU_C * (hidden + GELU_A * hidden * hidden * hidden)
    return 0.5 * hidden * (1.0 + jnp.tanh(inner_arg))


def gelu_slope(hidden):
    tangent = jnp.tanh(GELU_C * (hidden + GELU_A * hidden * hidden * hidden))
    return 0.5 * (1.0 + tangent) + 0.5 * hidden * (1.0 - tangent * tangent) * GELU_C * (
        1.0 + 3.0 * GELU_A * hidden * hidden
    )


def expert_rows(rows_x, rows_grad, up_local, down_local):
    hidden = jnp.dot(rows_x, up_local, preferred_element_type=jnp.float32)
    active = gelu_value(hidden).astype(jnp.bfloat16)
    out_part = jnp.dot(active, down_local, preferred_element_type=jnp.float32)
    d_active = lax.dot_general(
        rows_grad, down_local, (((1,), (1,)), ((), ())), preferred_element_type=jnp.float32
    )
    d_hidden = (d_active * gelu_slope(hidden)).astype(jnp.bfloat16)
    dx_part = lax.dot_general(
        d_hidden, up_local, (((1,), (1,)), ((), ())), preferred_element_type=jnp.float32
    )
    grad_down = lax.dot_general(
        active, rows_grad, (((0,), (0,)), ((), ())), preferred_element_type=jnp.float32
    )
    grad_up = lax.dot_general(
        rows_x, d_hidden, (((0,), (0,)), ((), ())), preferred_element_type=jnp.float32
    )
    return (out_part, dx_part, grad_up, grad_down)


def shards(tokens, routes, gates, upstream, w_up, w_down):
    tok_rows, feature_width = tokens.shape
    top_count = routes.shape[1]
    owners = lax.axis_size("expert")
    pair_count = lax.axis_size("tok")
    capacity = tok_rows * top_count // owners + max(1, tok_rows * top_count // (8 * owners))
    assigned = routes.reshape(-1)
    labels = jnp.arange(owners, dtype=jnp.int32)
    onehot = (assigned[:, None] == labels[None, :]).astype(jnp.int32)
    earlier = jnp.cumsum(onehot, axis=0) - onehot
    slot_rank = jnp.sum(earlier * onehot, axis=1)
    slot_of = assigned * capacity + slot_rank
    slot_ids = jnp.arange(owners * capacity, dtype=jnp.int32)
    matches = (slot_of[None, :] == slot_ids[:, None]).astype(jnp.int32)
    filled = jnp.sum(matches, axis=1) > 0
    source = jnp.sum(matches * jnp.arange(assigned.shape[0], dtype=jnp.int32)[None, :], axis=1)
    token_ids = source // top_count
    send_x = jnp.where(filled[:, None], tokens[token_ids], jnp.zeros((), jnp.bfloat16))
    gate_rows = jnp.where(filled, gates.reshape(-1)[source], jnp.zeros((), jnp.float32))
    send_grad = (gate_rows[:, None] * upstream[token_ids].astype(jnp.float32)).astype(jnp.bfloat16)
    send_x = send_x.reshape(owners, capacity, feature_width)
    send_grad = send_grad.reshape(owners, capacity, feature_width)
    recv_x, recv_grad = (
        lax.all_to_all(send_x, "expert", split_axis=0, concat_axis=0, tiled=True),
        lax.all_to_all(send_grad, "expert", split_axis=0, concat_axis=0, tiled=True),
    )
    both_x, both_grad = (
        lax.all_gather(recv_x[None], "tok", axis=0, tiled=True),
        lax.all_gather(recv_grad[None], "tok", axis=0, tiled=True),
    )
    rows_x = both_x.reshape(-1, feature_width)
    rows_grad = both_grad.reshape(-1, feature_width)
    out_part, dx_part, grad_up, grad_down = expert_rows(rows_x, rows_grad, w_up[0], w_down[0])
    shaped_out = out_part.reshape(pair_count, owners, capacity, feature_width)
    shaped_dx = dx_part.reshape(pair_count, owners, capacity, feature_width)
    summed_out, summed_dx = (
        lax.psum_scatter(shaped_out, "tok", scatter_dimension=0, tiled=True),
        lax.psum_scatter(shaped_dx, "tok", scatter_dimension=0, tiled=True),
    )
    home_out, home_dx = (
        lax.all_to_all(
            summed_out[0].astype(jnp.bfloat16), "expert", split_axis=0, concat_axis=0, tiled=True
        ),
        lax.all_to_all(
            summed_dx[0].astype(jnp.bfloat16), "expert", split_axis=0, concat_axis=0, tiled=True
        ),
    )
    out_pairs = (
        home_out.reshape(owners * capacity, feature_width)[slot_of]
        .reshape(tok_rows, top_count, feature_width)
        .astype(jnp.float32)
    )
    dx_pairs = (
        home_dx.reshape(owners * capacity, feature_width)[slot_of]
        .reshape(tok_rows, top_count, feature_width)
        .astype(jnp.float32)
    )
    mixed_out = jnp.sum(gates[:, :, None] * out_pairs, axis=1).astype(jnp.bfloat16)
    d_gates = jnp.sum(upstream.astype(jnp.float32)[:, None, :] * out_pairs, axis=2)
    d_tokens = jnp.sum(dx_pairs, axis=1).astype(jnp.bfloat16)
    return (
        mixed_out,
        d_tokens,
        d_gates,
        grad_up.astype(jnp.bfloat16)[None],
        grad_down.astype(jnp.bfloat16)[None],
    )


def solution(mesh):
    return jax.shard_map(
        shards,
        mesh=mesh,
        in_specs=(
            P(("expert", "tok"), None),
            P(("expert", "tok"), None),
            P(("expert", "tok"), None),
            P(("expert", "tok"), None),
            P("expert", None, "tok"),
            P("expert", "tok", None),
        ),
        out_specs=(
            P(("expert", "tok"), None),
            P(("expert", "tok"), None),
            P(("expert", "tok"), None),
            P("expert", None, "tok"),
            P("expert", "tok", None),
        ),
        check_vma=False,
    )
```

profile of v0, /device:TPU:14, one launch (start us, length us, event | category | flops | bytes accessed | tf_op | source)
XLA Modules:
  0.0 616.5 jit_solution(9409691657999771369)
XLA Ops:
  10.3 5.0 gather_fusion
  15.3 6.9 %gather.20 = bf16[16,36,3584]{2,1,0:T(8,128)(2,1)} reshape(bf16[576,3584]{1,0:T(8,128)(2,1)} %gather_fusion) | data formatting | bytes 8257536 | tf_op jit(solution)/shard_map/gather | solution.py:59
  26.9 7.3 %all-to-all-start = ((bf16[16,36,3584]{2,1,0:T(8,128)(2,1)}), bf16[16,36,3584]{2,1,0:T(8,128)(2,1)}, u32[]{:S(2)}, u32[]{:S(2)}) async-start(bf16[16,36,3584]{2,1,0:T(8,128)(2,1)} %broadcast_select_fusion), calls=%async_computation | async-start | bytes 9175040 | tf_op jit(solution)/shard_map/all_to_all | solution.py:65
  38.5 4.9 gather_fusion.3
  43.4 7.6 %reshape.211 = f32[16,36,3584]{2,1,0:T(8,128)} reshape(bf16[576,3584]{1,0:T(8,128)(2,1)} %gather_fusion.3) | data formatting | bytes 12386304 | tf_op jit(solution)/shard_map/convert_element_type | solution.py:61
  51.0 86.7 %all-to-all-done = bf16[16,36,3584]{2,1,0:T(8,128)(2,1)} async-done(((bf16[16,36,3584]{2,1,0:T(8,128)(2,1)}), bf16[16,36,3584]{2,1,0:T(8,128)(2,1)}, u32[]{:S(2)}, u32[]{:S(2)}) %all-to-all-start) | async-done | bytes 4128800 | tf_op jit(solution)/shard_map/all_to_all | solution.py:65
  137.7 5.4 copy.33
  148.1 104.5 %all_to_all.20 = bf16[16,36,3584]{2,1,0:T(8,128)(2,1)S(1)} all-to-all(bf16[16,36,3584]{2,1,0:T(8,128)(2,1)S(1)} %multiply_convert_fusion), channel_id=1, replica_groups=mesh['expert'=16,'tok'=2] {'expert'}, dimensions={0} | all-to-all | bytes 8257536 | tf_op jit(solution)/shard_map/all_to_all | solution.py:66
  256.1 12.7 %copy.34 = bf16[32,36,3584]{2,1,0:T(8,128)(2,1)} copy(bf16[32,36,3584]{2,0,1:T(8,128)(2,1)} %all-gather.5.cloned.1.call-done) | data formatting | bytes 16515072 | tf_op jit(solution)/shard_map/all_gather | solution.py:69
  268.8 12.7 %reshape.204 = bf16[1152,3584]{1,0:T(8,128)(2,1)} reshape(bf16[32,36,3584]{2,1,0:T(8,128)(2,1)} %copy.34) | data formatting | bytes 16515072 | tf_op jit(solution)/shard_map/reshape | solution.py:72
  281.5 11.4 %copy.38 = bf16[32,36,3584]{2,1,0:T(8,128)(2,1)} copy(bf16[32,36,3584]{2,0,1:T(8,128)(2,1)} %all-gather.7.cloned.1.call-done) | data formatting | bytes 16515072 | tf_op jit(solution)/shard_map/all_gather | solution.py:70
  292.9 12.6 %reshape.207 = bf16[1152,3584]{1,0:T(8,128)(2,1)} reshape(bf16[32,36,3584]{2,1,0:T(8,128)(2,1)} %copy.38) | data formatting | bytes 16515072 | tf_op jit(solution)/shard_map/reshape | solution.py:73
  305.5 10.6 %multiply_convert_fusion.1 = (bf16[1152,512]{1,0:T(8,128)(2,1)}, f32[1152,512]{1,0:T(8,128)S(1)}) fusion(bf16[1152,3584]{1,0:T(8,128)(2,1)} %reshape.204, bf16[1,3584,512]{2,1,0:T(8,128)(2,1)} %param.10), kind=kOutput, calls=%fused_computation.35 | convolution fusion | flops 4233166848 | bytes 15466496 | tf_op jit(solution)/shard_map/dot_general | solution.py:23
  316.1 5.8 fusion.15
  322.6 10.9 %fusion.4 = f32[2,16,36,3584]{3,2,1,0:T(8,128)} fusion(bf16[2,16,36,512]{3,2,1,0:T(8,128)(2,1)S(1)} %dot_general.26, bf16[1,3584,512]{2,1,0:T(8,128)(2,1)} %param.10), kind=kOutput, calls=%fused_computation.17 | convolution fusion | flops 4227858432 | bytes 21364736 | tf_op jit(solution)/shard_map/dot_general | solution.py:30
  335.7 14.5 %fusion.6 = f32[2,16,36,3584]{3,2,1,0:T(8,128)} fusion(bf16[2,16,36,512]{3,2,1,0:T(8,128)(2,1)S(1)} %dot_general.23, bf16[1,512,3584]{2,1,0:T(8,128)(2,1)} %param.11), kind=kOutput, calls=%fused_computation.19 | convolution fusion | flops 4227858432 | bytes 21364736 | tf_op jit(solution)/shard_map/dot_general | solution.py:25
  350.2 11.6 %reduce-scatter.5.cloned.1.call-done = f32[1,16,36,3584]{3,2,1,0:T(8,128)} async-done(((f32[2,16,36,3584]{3,2,1,0:T(8,128)}), f32[1,16,36,3584]{3,2,1,0:T(8,128)}) %reduce-scatter.5.cloned.1.call-update) | async-done | bytes 8257552 | tf_op jit(solution)/shard_map/reduce_scatter | solution.py:79
  361.8 6.3 %convert_bitcast_fusion = bf16[16,36,3584]{2,1,0:T(8,128)(2,1)} fusion(f32[1,16,36,3584]{3,2,1,0:T(8,128)} %reduce-scatter.5.cloned.1.call-done), kind=kLoop, calls=%fused_computation.14 | loop fusion | flops 2064384 | bytes 12386304 | tf_op jit(solution)/shard_map/convert_element_type | solution.py:86
  368.1 7.0 %all-to-all-start.3 = ((bf16[16,36,3584]{2,1,0:T(8,128)(2,1)}), bf16[16,36,3584]{2,1,0:T(8,128)(2,1)}, u32[]{:S(2)}, u32[]{:S(2)}) async-start(bf16[16,36,3584]{2,1,0:T(8,128)(2,1)} %convert_bitcast_fusion), calls=%async_computation.5 | async-start | bytes 9175040 | tf_op jit(solution)/shard_map/all_to_all | solution.py:85
  375.0 18.0 %reduce-scatter.3.cloned.1.call-done = f32[1,16,36,3584]{3,2,1,0:T(8,128)} async-done(((f32[2,16,36,3584]{3,2,1,0:T(8,128)}), f32[1,16,36,3584]{3,2,1,0:T(8,128)}) %reduce-scatter.3.cloned.1.call-update) | async-done | bytes 8257552 | tf_op jit(solution)/shard_map/reduce_scatter | solution.py:78
  393.0 6.2 %convert_bitcast_fusion.1 = bf16[16,36,3584]{2,1,0:T(8,128)(2,1)} fusion(f32[1,16,36,3584]{3,2,1,0:T(8,128)} %reduce-scatter.3.cloned.1.call-done), kind=kLoop, calls=%fused_computation.15 | loop fusion | flops 2064384 | bytes 12386304 | tf_op jit(solution)/shard_map/convert_element_type | solution.py:83
  399.2 80.1 %all-to-all-done.3 = bf16[16,36,3584]{2,1,0:T(8,128)(2,1)} async-done(((bf16[16,36,3584]{2,1,0:T(8,128)(2,1)}), bf16[16,36,3584]{2,1,0:T(8,128)(2,1)}, u32[]{:S(2)}, u32[]{:S(2)}) %all-to-all-start.3) | async-done | bytes 4128800 | tf_op jit(solution)/shard_map/all_to_all | solution.py:85
  479.2 5.4 all-to-all-start.1
  484.9 10.5 %fusion.3 = bf16[1,512,3584]{2,1,0:T(8,128)(2,1)} fusion(bf16[1152,512]{1,0:T(8,128)(2,1)} %get-tuple-element.21, bf16[1152,3584]{1,0:T(8,128)(2,1)} %reshape.207), kind=kOutput, calls=%fused_computation.13 | convolution fusion | flops 4229693440 | bytes 13107200 | tf_op jit(solution)/shard_map/dot_general | solution.py:33
  495.4 9.8 %fusion.2 = bf16[1,3584,512]{2,1,0:T(8,128)(2,1)} fusion(bf16[1152,3584]{1,0:T(8,128)(2,1)} %reshape.204, bf16[1152,512]{1,0:T(8,128)(2,1)S(1)} %fusion.15), kind=kOutput, calls=%fused_computation.12 | convolution fusion | flops 4229693440 | bytes 13107200 | tf_op jit(solution)/shard_map/dot_general | solution.py:36
  505.2 6.9 %reshape.208 = bf16[576,3584]{1,0:T(8,128)(2,1)} reshape(bf16[16,36,3584]{2,1,0:T(8,128)(2,1)} %all-to-all-done.3) | data formatting | bytes 8257536 | tf_op jit(solution)/shard_map/reshape | solution.py:95
  512.1 10.7 %gather_fusion.4 = bf16[512,3584]{1,0:T(8,128)(2,1)} fusion(bf16[576,3584]{1,0:T(8,128)(2,1)} %reshape.208, s32[1024]{0:T(1024)S(1)} %pad_clamp_fusion.1), kind=kCustom, calls=%fused_computation.4 | custom fusion | bytes 7342080 | tf_op jit(solution)/shard_map/gather | solution.py:95
  522.9 5.3 bitcast_reduce_fusion
  528.2 57.7 %all-to-all-done.1 = bf16[16,36,3584]{2,1,0:T(8,128)(2,1)} async-done(((bf16[16,36,3584]{2,1,0:T(8,128)(2,1)}), bf16[16,36,3584]{2,1,0:T(8,128)(2,1)}, u32[]{:S(2)}, u32[]{:S(2)}) %all-to-all-start.1) | async-done | bytes 4128800 | tf_op jit(solution)/shard_map/all_to_all | solution.py:82
  585.9 6.9 %reshape.205 = bf16[576,3584]{1,0:T(8,128)(2,1)} reshape(bf16[16,36,3584]{2,1,0:T(8,128)(2,1)} %all-to-all-done.1) | data formatting | bytes 8257536 | tf_op jit(solution)/shard_map/reshape | solution.py:90
  592.8 10.7 %gather_fusion.1 = bf16[512,3584]{1,0:T(8,128)(2,1)} fusion(bf16[576,3584]{1,0:T(8,128)(2,1)} %reshape.205, s32[1024]{0:T(1024)S(1)} %pad_clamp_fusion.1), kind=kCustom, calls=%fused_computation.1 | custom fusion | bytes 7342080 | tf_op jit(solution)/shard_map/gather | solution.py:90
  603.5 5.6 fusion.1
  (60 shorter events, 24.2 us)
Async XLA Ops:
  7.2 3.1 copy-start
  26.9 7.3 %copy-start.7 = (f32[64,8]{0,1:T(8,128)S(1)}, f32[64,8]{0,1:T(8,128)}, u32[]{:S(2)}) copy-start(f32[64,8]{0,1:T(8,128)} %param.8) | copy-start | bytes 6148
  26.9 110.8 %all-to-all-start = ((bf16[16,36,3584]{2,1,0:T(8,128)(2,1)}), bf16[16,36,3584]{2,1,0:T(8,128)(2,1)}, u32[]{:S(2)}, u32[]{:S(2)}) async-start(bf16[16,36,3584]{2,1,0:T(8,128)(2,1)} %broadcast_select_fusion), calls=%async_computation | async-start | bytes 9175040 | tf_op jit(solution)/shard_map/all_to_all | solution.py:65
  34.2 4.3 copy-start.2
  34.2 221.9 %all-gather.5.cloned.1.call-start = ((), (), s32[]{:S(2)}) async-start(), calls=%async_computation.8 | async-start | bytes 12386304 | tf_op jit(solution)/shard_map/all_gather | solution.py:69
  34.3 9.1 %copy-start.4 = (f32[64,8]{1,0:T(8,128)}, f32[64,8]{1,0:T(8,128)S(1)}, u32[]{:S(2)}) copy-start(f32[64,8]{1,0:T(8,128)S(1)} %copy.29) | copy-start | bytes 6148
  143.2 138.3 %all-gather.7.cloned.1.call-start = ((), (), s32[]{:S(2)}) async-start(), calls=%async_computation.9 | async-start | bytes 12386304 | tf_op jit(solution)/shard_map/all_gather | solution.py:70
  255.8 106.0 %reduce-scatter.5.cloned.1.call-start = ((), (), s32[]{:S(2)}) async-start(), calls=%async_computation.7 | async-start | bytes 27525120 | tf_op jit(solution)/shard_map/reduce_scatter | solution.py:79
  305.5 10.6 %copy-start.3 = (bf16[1152,3584]{1,0:T(8,128)(2,1)S(1)}, bf16[1152,3584]{1,0:T(8,128)(2,1)}, u32[]{:S(2)}) copy-start(bf16[1152,3584]{1,0:T(8,128)(2,1)} %reshape.207) | copy-start | bytes 24772612
  305.5 10.6 %copy-start.8 = (bf16[1,512,3584]{2,1,0:T(8,128)(2,1)S(1)}, bf16[1,512,3584]{2,1,0:T(8,128)(2,1)}, u32[]{:S(2)}) copy-start(bf16[1,512,3584]{2,1,0:T(8,128)(2,1)} %param.11) | copy-start | bytes 11010052
  333.5 59.5 %reduce-scatter.3.cloned.1.call-start = ((), (), s32[]{:S(2)}) async-start(), calls=%async_computation.6 | async-start | bytes 27525120 | tf_op jit(solution)/shard_map/reduce_scatter | solution.py:78
  368.1 111.1 %all-to-all-start.3 = ((bf16[16,36,3584]{2,1,0:T(8,128)(2,1)}), bf16[16,36,3584]{2,1,0:T(8,128)(2,1)}, u32[]{:S(2)}, u32[]{:S(2)}) async-start(bf16[16,36,3584]{2,1,0:T(8,128)(2,1)} %convert_bitcast_fusion), calls=%async_computation.5 | async-start | bytes 9175040 | tf_op jit(solution)/shard_map/all_to_all | solution.py:85
  399.2 85.5 %copy-start.6 = (s32[64,8]{0,1:T(8,128)S(1)}, s32[64,8]{0,1:T(8,128)}, u32[]{:S(2)}) copy-start(s32[64,8]{0,1:T(8,128)} %param.7) | copy-start | bytes 6148
  479.2 106.7 %all-to-all-start.1 = ((bf16[16,36,3584]{2,1,0:T(8,128)(2,1)}), bf16[16,36,3584]{2,1,0:T(8,128)(2,1)}, u32[]{:S(2)}, u32[]{:S(2)}) async-start(bf16[16,36,3584]{2,1,0:T(8,128)(2,1)} %convert_bitcast_fusion.1), calls=%async_computation.2 | async-start | bytes 9175040 | tf_op jit(solution)/shard_map/all_to_all | solution.py:82
  592.8 10.7 %copy-start.5 = (f32[64,8]{1,0:T(8,128)S(1)}, f32[64,8]{1,0:T(8,128)}, u32[]{:S(2)}) copy-start(f32[64,8]{1,0:T(8,128)} %copy-done.4) | copy-start | bytes 6148
  592.8 16.9 %copy-start.1 = (bf16[64,3584]{1,0:T(8,128)(2,1)S(1)}, bf16[64,3584]{1,0:T(8,128)(2,1)}, u32[]{:S(2)}) copy-start(bf16[64,3584]{1,0:T(8,128)(2,1)} %param.6) | copy-start | bytes 1376260
Sparse Core Ops, SparseCore 0:
  143.3 18.9 all-gather.4
  256.0 19.9 all-gather.6
  333.6 28.1 reduce-scatter.4
  364.0 28.9 reduce-scatter.2
where the time goes:
time: 625 us; the launch traced here: 616 us
  waiting for transfers between devices  254 us (41%)
  local copies, waits for them, and re-layouts  127 us (20%)
  blocking collectives  105 us (17%)
  matrix products  62.1 us (10%)
  other arithmetic  34.7 us (6%)
  starting transfers between devices  20 us (3%)
  between operations  14.2 us (2%)
    all_to_all x1, blocking collectives, shards(): lax.all_to_all(send_grad, 'expert', split_axis=0, concat_axis=0, tiled=True)  105 us
    all_to_all x1, waiting for transfers between devices, shards(): lax.all_to_all(send_x, 'expert', split_axis=0, concat_axis=0, tiled=True)  86.7 us
    all_to_all x1, waiting for transfers between devices, shards(): lax.all_to_all(summed_dx[0].astype(jnp.bfloat16), 'expert', split_axis=0,...  80.1 us
    all_to_all x1, waiting for transfers between devices, shards(): lax.all_to_all(summed_out[0].astype(jnp.bfloat16), 'expert', split_axis=0...  57.7 us
    reduce_scatter x1, waiting for transfers between devices, shards(): lax.psum_scatter(shaped_out, 'tok', scatter_dimension=0, tiled=True)  18 us
    dot_general x1, matrix products, expert_rows(): out_part = jnp.dot(active, down_local, preferred_element_type=jnp.float32)  14.5 us
    all_gather x1, local copies, waits for them, and re-layouts, shards(): lax.all_gather(recv_x[None], 'tok', axis=0, tiled=True)  12.7 us
    reshape x1, local copies, waits for them, and re-layouts, shards(): rows_x = both_x.reshape(-1, feature_width)  12.7 us
  transfers between devices with their start and end apart: 7, of which 5 were waited for; matrix products, arithmetic and copies ran while one was open for 20% of the time, Pallas kernels for 0%

commit v1 on v0

--- a/solution.py
+++ b/solution.py
@@ -5,6 +5,18 @@
 
 GELU_C = 0.7978845608028654
 GELU_A = 0.044715
+
+
+def sent_to_each(value, axis, split, join):
+    ways, here = (lax.axis_size(axis), lax.axis_index(axis))
+    width = value.shape[split] // ways
+    turned = jnp.roll(value, -here * width, axis=split)
+    got = [lax.slice_in_dim(turned, 0, width, axis=split)]
+    for far in range(1, ways):
+        sent = lax.slice_in_dim(turned, far * width, (far + 1) * width, axis=split)
+        got.append(lax.ppermute(sent, axis, [(d, (d + far) % ways) for d in range(ways)]))
+    line = jnp.concatenate(got[::-1], axis=join)
+    return jnp.roll(line, (here + 1) * got[0].shape[join], axis=join)
 
 
 def gelu_value(hidden):
@@ -62,7 +74,7 @@
     send_x = send_x.reshape(owners, capacity, feature_width)
     send_grad = send_grad.reshape(owners, capacity, feature_width)
     recv_x, recv_grad = (
-        lax.all_to_all(send_x, "expert", split_axis=0, concat_axis=0, tiled=True),
+        sent_to_each(send_x, "expert", 0, 0),
         lax.all_to_all(send_grad, "expert", split_axis=0, concat_axis=0, tiled=True),
     )
     both_x, both_grad = (

time: 625 us -> 663 us (1.061)
  starting transfers between devices: 20 us -> 74.5 us
  waiting for transfers between devices: 254 us -> 225 us
    all_to_all x1 -> x0, waiting for transfers between devices: 86.7 us -> none  [shards(): lax.all_to_all(send_x, 'expert', split_axis=0, concat_axis=0, tiled=True)]
    ppermute x0 -> x15, waiting for transfers between devices: none -> 72.6 us  [sent_to_each(): lax.ppermute(sent, axis, [(d, (d + far) % ways) for d in range(ways)])]
    ppermute x0 -> x15, starting transfers between devices: none -> 61.7 us  [sent_to_each(): lax.ppermute(sent, axis, [(d, (d + far) % ways) for d in range(ways)])]
    all_to_all x1, waiting for transfers between devices: 80.1 us -> 57.6 us  [shards(): lax.all_to_all(summed_dx[0].astype(jnp.bfloat16), 'expert', split_axis=0,...]
    all_to_all x1, waiting for transfers between devices: 57.7 us -> 79.2 us  [shards(): lax.all_to_all(summed_out[0].astype(jnp.bfloat16), 'expert', split_axis=0...]
    reduce_scatter x1, waiting for transfers between devices: 18 us -> 0.02 us  [shards(): lax.psum_scatter(shaped_out, 'tok', scatter_dimension=0, tiled=True)]
    all_to_all x1 -> x0, starting transfers between devices: 7.27 us -> none  [shards(): lax.all_to_all(send_x, 'expert', split_axis=0, concat_axis=0, tiled=True)]
  transfers between devices with their start and end apart: 7 -> 21, of which waited for: 5 -> 13; matrix products, arithmetic and copies ran while one was open for 20% -> 28% of each run, Pallas kernels for 0% -> 0%
where the time goes in v1:
time: 663 us; the launch traced here: 655 us
  waiting for transfers between devices  225 us (34%)
  local copies, waits for them, and re-layouts  133 us (20%)
  blocking collectives  107 us (16%)
  starting transfers between devices  74.5 us (11%)
  matrix products  64.1 us (10%)
  other arithmetic  36.2 us (5%)
  between operations  14.6 us (2%)
    all_to_all x1, blocking collectives, shards(): lax.all_to_all(send_grad, 'expert', split_axis=0, concat_axis=0, tiled=True)  107 us
    all_to_all x1, waiting for transfers between devices, shards(): lax.all_to_all(summed_out[0].astype(jnp.bfloat16), 'expert', split_axis=0...  79.2 us
    ppermute x15, waiting for transfers between devices, sent_to_each(): lax.ppermute(sent, axis, [(d, (d + far) % ways) for d in range(ways)])  72.6 us
    ppermute x15, starting transfers between devices, sent_to_each(): lax.ppermute(sent, axis, [(d, (d + far) % ways) for d in range(ways)])  61.7 us
    all_to_all x1, waiting for transfers between devices, shards(): lax.all_to_all(summed_dx[0].astype(jnp.bfloat16), 'expert', split_axis=0,...  57.6 us
    reduce_scatter x1, waiting for transfers between devices, shards(): lax.psum_scatter(shaped_dx, 'tok', scatter_dimension=0, tiled=True)  15.1 us
    reshape x1, local copies, waits for them, and re-layouts, shards(): rows_grad = both_grad.reshape(-1, feature_width)  13.8 us
    all_gather x1, local copies, waits for them, and re-layouts, shards(): lax.all_gather(recv_grad[None], 'tok', axis=0, tiled=True)  13.5 us
  transfers between devices with their start and end apart: 21, of which 13 were waited for; matrix products, arithmetic and copies ran while one was open for 28% of the time, Pallas kernels for 0%

profile of v1, /device:TPU:14, one launch (start us, length us, event | category | flops | bytes accessed | tf_op | source)
XLA Modules:
  0.0 654.8 jit_solution(5750851344823024086)
XLA Ops:
  16.0 6.9 %gather.20 = bf16[16,36,3584]{2,1,0:T(8,128)(2,1)} reshape(bf16[576,3584]{1,0:T(8,128)(2,1)} %gather_fusion) | data formatting | bytes 8257536 | tf_op jit(solution)/shard_map/gather | solution.py:71
  49.1 7.6 %reshape.211 = f32[16,36,3584]{2,1,0:T(8,128)} reshape(bf16[576,3584]{1,0:T(8,128)(2,1)} %gather_fusion.3) | data formatting | bytes 12386304 | tf_op jit(solution)/shard_map/convert_element_type | solution.py:73
  56.7 8.5 %collective-permute-done.1 = bf16[1,36,3584]{2,1,0:T(8,128)(2,1)S(1)} collective-permute-done((bf16[1,36,3584]{2,1,0:T(8,128)(2,1)}, bf16[1,36,3584]{2,1,0:T(8,128)(2,1)S(1)}, u32[]{:S(2)}, u32[]{:S(2)}) %collective-permute-start.1) | collective-permute-done | bytes 258080 | tf_op jit(solution)/shard_map/ppermute | solution.py:17
  66.8 6.3 collective-permute-done.2
  80.8 6.5 collective-permute-start.4
  91.7 8.4 %collective-permute-start.5 = (bf16[1,36,3584]{2,1,0:T(8,128)(2,1)}, bf16[1,36,3584]{2,1,0:T(8,128)(2,1)S(1)}, u32[]{:S(2)}, u32[]{:S(2)}) collective-permute-start(bf16[1,36,3584]{2,1,0:T(8,128)(2,1)} %get-tuple-element.31), channel_id=1, source_target_pairs={{0,20},{2,22},{4,24},{6,26},{8,28},{10,30},{12,0},{14,2},{16,4},{1... | collective-permute-start | bytes 774152 | tf_op jit(solution)/shard_map/ppermute | solution.py:17
  109.2 6.6 %collective-permute-done.6 = bf16[1,36,3584]{2,1,0:T(8,128)(2,1)S(1)} collective-permute-done((bf16[1,36,3584]{2,1,0:T(8,128)(2,1)}, bf16[1,36,3584]{2,1,0:T(8,128)(2,1)S(1)}, u32[]{:S(2)}, u32[]{:S(2)}) %collective-permute-start.6) | collective-permute-done | bytes 258080 | tf_op jit(solution)/shard_map/ppermute | solution.py:17
  115.8 27.1 %collective-permute-start.7 = (bf16[1,36,3584]{2,1,0:T(8,128)(2,1)S(1)}, bf16[1,36,3584]{2,1,0:T(8,128)(2,1)S(1)}, u32[]{:S(2)}, u32[]{:S(2)}) collective-permute-start(bf16[1,36,3584]{2,1,0:T(8,128)(2,1)S(1)} %get-tuple-element.29), channel_id=1, source_target_pairs={{0,16},{2,18},{4,20},{6,22},{8,24},{10,26},{12,28},{14,30},{16,0},... | collective-permute-start | bytes 774152 | tf_op jit(solution)/shard_map/ppermute | solution.py:17
  148.8 13.5 %collective-permute-done.8 = bf16[1,36,3584]{2,1,0:T(8,128)(2,1)S(1)} collective-permute-done((bf16[1,36,3584]{2,1,0:T(8,128)(2,1)}, bf16[1,36,3584]{2,1,0:T(8,128)(2,1)S(1)}, u32[]{:S(2)}, u32[]{:S(2)}) %collective-permute-start.8) | collective-permute-done | bytes 258080 | tf_op jit(solution)/shard_map/ppermute | solution.py:17
  162.3 7.5 %collective-permute-done.9 = bf16[1,36,3584]{2,1,0:T(8,128)(2,1)S(1)} collective-permute-done((bf16[1,36,3584]{2,1,0:T(8,128)(2,1)S(1)}, bf16[1,36,3584]{2,1,0:T(8,128)(2,1)S(1)}, u32[]{:S(2)}, u32[]{:S(2)}) %collective-permute-start.9) | collective-permute-done | bytes 258080 | tf_op jit(solution)/shard_map/ppermute | solution.py:17
  173.3 9.2 %collective-permute-done.10 = bf16[1,36,3584]{2,1,0:T(8,128)(2,1)S(1)} collective-permute-done((bf16[1,36,3584]{2,1,0:T(8,128)(2,1)S(1)}, bf16[1,36,3584]{2,1,0:T(8,128)(2,1)S(1)}, u32[]{:S(2)}, u32[]{:S(2)}) %collective-permute-start.10) | collective-permute-done | bytes 258080 | tf_op jit(solution)/shard_map/ppermute | solution.py:17
  193.6 107.3 %all_to_all.15 = bf16[16,36,3584]{2,1,0:T(8,128)(2,1)S(1)} all-to-all(bf16[16,36,3584]{2,1,0:T(8,128)(2,1)S(1)} %multiply_convert_fusion), channel_id=1, replica_groups=mesh['expert'=16,'tok'=2] {'expert'}, dimensions={0} | all-to-all | bytes 8257536 | tf_op jit(solution)/shard_map/all_to_all | solution.py:78
  304.7 12.7 %copy.34 = bf16[32,36,3584]{2,1,0:T(8,128)(2,1)} copy(bf16[32,36,3584]{2,0,1:T(8,128)(2,1)} %all-gather.5.cloned.1.call-done) | data formatting | bytes 16515072 | tf_op jit(solution)/shard_map/all_gather | solution.py:81
  317.4 12.7 %reshape.204 = bf16[1152,3584]{1,0:T(8,128)(2,1)} reshape(bf16[32,36,3584]{2,1,0:T(8,128)(2,1)} %copy.34) | data formatting | bytes 16515072 | tf_op jit(solution)/shard_map/reshape | solution.py:84
  330.1 10.8 %multiply_convert_fusion.1 = (bf16[1152,512]{1,0:T(8,128)(2,1)S(1)}, f32[1152,512]{1,0:T(8,128)}) fusion(bf16[1152,3584]{1,0:T(8,128)(2,1)} %reshape.204, bf16[1,3584,512]{2,1,0:T(8,128)(2,1)} %param.12), kind=kOutput, calls=%fused_computation.41 | convolution fusion | flops 4233166848 | bytes 15466496 | tf_op jit(solution)/shard_map/dot_general | solution.py:35
  341.1 10.9 %fusion.8 = f32[2,16,36,3584]{3,2,1,0:T(8,128)} fusion(bf16[2,16,36,512]{3,2,1,0:T(8,128)(2,1)S(1)} %dot_general.23, bf16[1,512,3584]{2,1,0:T(8,128)(2,1)} %param.13), kind=kOutput, calls=%fused_computation.25 | convolution fusion | flops 4227858432 | bytes 21364736 | tf_op jit(solution)/shard_map/dot_general | solution.py:37
  352.3 13.5 %copy.38 = bf16[32,36,3584]{2,1,0:T(8,128)(2,1)} copy(bf16[32,36,3584]{2,0,1:T(8,128)(2,1)} %all-gather.7.cloned.1.call-done) | data formatting | bytes 16515072 | tf_op jit(solution)/shard_map/all_gather | solution.py:82
  365.8 13.8 %reshape.207 = bf16[1152,3584]{1,0:T(8,128)(2,1)} reshape(bf16[32,36,3584]{2,1,0:T(8,128)(2,1)} %copy.38) | data formatting | bytes 16515072 | tf_op jit(solution)/shard_map/reshape | solution.py:85
  379.6 11.9 %fusion.17 = bf16[1152,512]{1,0:T(8,128)(2,1)} fusion(bf16[1152,3584]{1,0:T(8,128)(2,1)} %reshape.207, bf16[1,512,3584]{2,1,0:T(8,128)(2,1)} %param.13, f32[1152,512]{1,0:T(8,128)} %get-tuple-element.38), kind=kOutput, calls=%fused_computation.35 | convolution fusion | flops 4239065088 | bytes 15466496 | tf_op jit(solution)/shard_map/dot_general | solution.py:38
  393.6 10.9 %fusion.6 = f32[2,16,36,3584]{3,2,1,0:T(8,128)} fusion(bf16[2,16,36,512]{3,2,1,0:T(8,128)(2,1)S(1)} %dot_general.26, bf16[1,3584,512]{2,1,0:T(8,128)(2,1)} %param.12), kind=kOutput, calls=%fused_computation.23 | convolution fusion | flops 4227858432 | bytes 21364736 | tf_op jit(solution)/shard_map/dot_general | solution.py:42
  404.6 6.2 convert_bitcast_fusion.1
  410.8 6.9 %all-to-all-start = ((bf16[16,36,3584]{2,1,0:T(8,128)(2,1)}), bf16[16,36,3584]{2,1,0:T(8,128)(2,1)}, u32[]{:S(2)}, u32[]{:S(2)}) async-start(bf16[16,36,3584]{2,1,0:T(8,128)(2,1)} %convert_bitcast_fusion.1), calls=%async_computation.1 | async-start | bytes 9175040 | tf_op jit(solution)/shard_map/all_to_all | solution.py:94
  417.7 15.1 %reduce-scatter.5.cloned.1.call-done = f32[1,16,36,3584]{3,2,1,0:T(8,128)} async-done(((f32[2,16,36,3584]{3,2,1,0:T(8,128)}), f32[1,16,36,3584]{3,2,1,0:T(8,128)}) %reduce-scatter.5.cloned.1.call-update) | async-done | bytes 8257552 | tf_op jit(solution)/shard_map/reduce_scatter | solution.py:91
  432.8 6.2 convert_bitcast_fusion
  439.0 79.2 %all-to-all-done = bf16[16,36,3584]{2,1,0:T(8,128)(2,1)} async-done(((bf16[16,36,3584]{2,1,0:T(8,128)(2,1)}), bf16[16,36,3584]{2,1,0:T(8,128)(2,1)}, u32[]{:S(2)}, u32[]{:S(2)}) %all-to-all-start) | async-done | bytes 4128800 | tf_op jit(solution)/shard_map/all_to_all | solution.py:94
  523.7 9.9 %fusion.3 = bf16[1,512,3584]{2,1,0:T(8,128)(2,1)} fusion(bf16[1152,512]{1,0:T(8,128)(2,1)S(1)} %get-tuple-element.37, bf16[1152,3584]{1,0:T(8,128)(2,1)} %reshape.207), kind=kOutput, calls=%fused_computation.17 | convolution fusion | flops 4229693440 | bytes 13107200 | tf_op jit(solution)/shard_map/dot_general | solution.py:45
  533.6 9.8 %fusion.2 = bf16[1,3584,512]{2,1,0:T(8,128)(2,1)} fusion(bf16[1152,3584]{1,0:T(8,128)(2,1)} %reshape.204, bf16[1152,512]{1,0:T(8,128)(2,1)S(1)} %copy-done.4), kind=kOutput, calls=%fused_computation.16 | convolution fusion | flops 4229693440 | bytes 13107200 | tf_op jit(solution)/shard_map/dot_general | solution.py:48
  543.3 6.9 %reshape.205 = bf16[576,3584]{1,0:T(8,128)(2,1)} reshape(bf16[16,36,3584]{2,1,0:T(8,128)(2,1)} %all-to-all-done) | data formatting | bytes 8257536 | tf_op jit(solution)/shard_map/reshape | solution.py:102
  550.3 10.6 %gather_fusion.1 = bf16[512,3584]{1,0:T(8,128)(2,1)} fusion(bf16[576,3584]{1,0:T(8,128)(2,1)} %reshape.205, s32[1024]{0:T(1024)S(1)} %pad_clamp_fusion.1), kind=kCustom, calls=%fused_computation.1 | custom fusion | bytes 7342080 | tf_op jit(solution)/shard_map/gather | solution.py:102
  567.2 57.6 %all-to-all-done.2 = bf16[16,36,3584]{2,1,0:T(8,128)(2,1)} async-done(((bf16[16,36,3584]{2,1,0:T(8,128)(2,1)}), bf16[16,36,3584]{2,1,0:T(8,128)(2,1)}, u32[]{:S(2)}, u32[]{:S(2)}) %all-to-all-start.2) | async-done | bytes 4128800 | tf_op jit(solution)/shard_map/all_to_all | solution.py:97
  624.7 6.9 %reshape.208 = bf16[576,3584]{1,0:T(8,128)(2,1)} reshape(bf16[16,36,3584]{2,1,0:T(8,128)(2,1)} %all-to-all-done.2) | data formatting | bytes 8257536 | tf_op jit(solution)/shard_map/reshape | solution.py:107
  631.7 10.9 %gather_fusion.4 = bf16[512,3584]{1,0:T(8,128)(2,1)} fusion(bf16[576,3584]{1,0:T(8,128)(2,1)} %reshape.208, s32[1024]{0:T(1024)S(1)} %pad_clamp_fusion.1), kind=kCustom, calls=%fused_computation.4 | custom fusion | bytes 7342080 | tf_op jit(solution)/shard_map/gather | solution.py:107
  (111 shorter events, 101.4 us)
Async XLA Ops:
  7.2 3.8 copy-start
  7.2 297.5 %all-gather.5.cloned.1.call-start = ((), (), s32[]{:S(2)}) async-start(), calls=%async_computation.7 | async-start | bytes 12386304 | tf_op jit(solution)/shard_map/all_gather | solution.py:81
  9.8 0.6 copy-start.7
  27.3 2.2 copy-start.3
  29.5 10.4 %copy-start.10 = (f32[64,8]{0,1:T(8,128)S(1)}, f32[64,8]{0,1:T(8,128)}, u32[]{:S(2)}) copy-start(f32[64,8]{0,1:T(8,128)} %param.10) | copy-start | bytes 6148
  29.5 14.6 %copy-start.2 = (bf16[64,3584]{1,0:T(8,128)(2,1)S(1)}, bf16[64,3584]{1,0:T(8,128)(2,1)}, u32[]{:S(2)}) copy-start(bf16[64,3584]{1,0:T(8,128)(2,1)} %param.11) | copy-start | bytes 1376260
  31.1 25.5 %collective-permute-start = (bf16[1,36,3584]{2,1,0:T(8,128)(2,1)S(1)}, bf16[1,36,3584]{2,1,0:T(8,128)(2,1)S(1)}, u32[]{:S(2)}, u32[]{:S(2)}) collective-permute-start(bf16[1,36,3584]{2,1,0:T(8,128)(2,1)S(1)} %get-tuple-element.36), channel_id=1, source_target_pairs={{0,30},{2,0},{4,2},{6,4},{8,6},{10,8},{12,10},{14,12},{16,14},{18,... | collective-permute-start | bytes 774152 | tf_op jit(solution)/shard_map/ppermute | solution.py:17
  31.7 151.0 %collective-permute-start.14 = (bf16[1,36,3584]{2,1,0:T(8,128)(2,1)S(1)}, bf16[1,36,3584]{2,1,0:T(8,128)(2,1)S(1)}, u32[]{:S(2)}, u32[]{:S(2)}) collective-permute-start(bf16[1,36,3584]{2,1,0:T(8,128)(2,1)S(1)} %get-tuple-element.22), channel_id=1, source_target_pairs={{0,2},{2,4},{4,6},{6,8},{8,10},{10,12},{12,14},{14,16},{16,18},{18... | collective-permute-start | bytes 774152 | tf_op jit(solution)/shard_map/ppermute | solution.py:17
  34.9 147.7 %collective-permute-start.13 = (bf16[1,36,3584]{2,1,0:T(8,128)(2,1)S(1)}, bf16[1,36,3584]{2,1,0:T(8,128)(2,1)S(1)}, u32[]{:S(2)}, u32[]{:S(2)}) collective-permute-start(bf16[1,36,3584]{2,1,0:T(8,128)(2,1)S(1)} %get-tuple-element.23), channel_id=1, source_target_pairs={{0,4},{2,6},{4,8},{6,10},{8,12},{10,14},{12,16},{14,18},{16,20},{1... | collective-permute-start | bytes 774152 | tf_op jit(solution)/shard_map/ppermute | solution.py:17
  35.6 147.0 %collective-permute-start.12 = (bf16[1,36,3584]{2,1,0:T(8,128)(2,1)S(1)}, bf16[1,36,3584]{2,1,0:T(8,128)(2,1)S(1)}, u32[]{:S(2)}, u32[]{:S(2)}) collective-permute-start(bf16[1,36,3584]{2,1,0:T(8,128)(2,1)S(1)} %get-tuple-element.24), channel_id=1, source_target_pairs={{0,6},{2,8},{4,10},{6,12},{8,14},{10,16},{12,18},{14,20},{16,22},{... | collective-permute-start | bytes 774152 | tf_op jit(solution)/shard_map/ppermute | solution.py:17
  36.5 146.0 %collective-permute-start.11 = (bf16[1,36,3584]{2,1,0:T(8,128)(2,1)}, bf16[1,36,3584]{2,1,0:T(8,128)(2,1)S(1)}, u32[]{:S(2)}, u32[]{:S(2)}) collective-permute-start(bf16[1,36,3584]{2,1,0:T(8,128)(2,1)} %get-tuple-element.25), channel_id=1, source_target_pairs={{0,8},{2,10},{4,12},{6,14},{8,16},{10,18},{12,20},{14,22},{16,24},... | collective-permute-start | bytes 774152 | tf_op jit(solution)/shard_map/ppermute | solution.py:17
  56.6 105.7 %copy-start.6 = (bf16[1,36,3584]{2,1,0:T(8,128)(2,1)S(1)}, bf16[1,36,3584]{2,1,0:T(8,128)(2,1)}, u32[]{:S(2)}) copy-start(bf16[1,36,3584]{2,1,0:T(8,128)(2,1)} %get-tuple-element.27) | copy-start | bytes 774148
  56.6 113.2 %copy-start.5 = (bf16[1,36,3584]{2,1,0:T(8,128)(2,1)S(1)}, bf16[1,36,3584]{2,1,0:T(8,128)(2,1)}, u32[]{:S(2)}) copy-start(bf16[1,36,3584]{2,1,0:T(8,128)(2,1)} %get-tuple-element.26) | copy-start | bytes 774148
  56.6 8.6 %collective-permute-start.1 = (bf16[1,36,3584]{2,1,0:T(8,128)(2,1)}, bf16[1,36,3584]{2,1,0:T(8,128)(2,1)S(1)}, u32[]{:S(2)}, u32[]{:S(2)}) collective-permute-start(bf16[1,36,3584]{2,1,0:T(8,128)(2,1)} %get-tuple-element.35), channel_id=1, source_target_pairs={{0,28},{2,30},{4,0},{6,2},{8,4},{10,6},{12,8},{14,10},{16,12},{18,... | collective-permute-start | bytes 774152 | tf_op jit(solution)/shard_map/ppermute | solution.py:17
  65.3 7.7 %collective-permute-start.2 = (bf16[1,36,3584]{2,1,0:T(8,128)(2,1)}, bf16[1,36,3584]{2,1,0:T(8,128)(2,1)S(1)}, u32[]{:S(2)}, u32[]{:S(2)}) collective-permute-start(bf16[1,36,3584]{2,1,0:T(8,128)(2,1)} %get-tuple-element.34), channel_id=1, source_target_pairs={{0,26},{2,28},{4,30},{6,0},{8,2},{10,4},{12,6},{14,8},{16,10},{18,... | collective-permute-start | bytes 774152 | tf_op jit(solution)/shard_map/ppermute | solution.py:17
  73.0 7.8 %collective-permute-start.3 = (bf16[1,36,3584]{2,1,0:T(8,128)(2,1)}, bf16[1,36,3584]{2,1,0:T(8,128)(2,1)S(1)}, u32[]{:S(2)}, u32[]{:S(2)}) collective-permute-start(bf16[1,36,3584]{2,1,0:T(8,128)(2,1)} %get-tuple-element.33), channel_id=1, source_target_pairs={{0,24},{2,26},{4,28},{6,30},{8,0},{10,2},{12,4},{14,6},{16,8},{18,... | collective-permute-start | bytes 774152 | tf_op jit(solution)/shard_map/ppermute | solution.py:17
  80.8 10.9 %collective-permute-start.4 = (bf16[1,36,3584]{2,1,0:T(8,128)(2,1)}, bf16[1,36,3584]{2,1,0:T(8,128)(2,1)S(1)}, u32[]{:S(2)}, u32[]{:S(2)}) collective-permute-start(bf16[1,36,3584]{2,1,0:T(8,128)(2,1)} %get-tuple-element.32), channel_id=1, source_target_pairs={{0,22},{2,24},{4,26},{6,28},{8,30},{10,0},{12,2},{14,4},{16,6},{18... | collective-permute-start | bytes 774152 | tf_op jit(solution)/shard_map/ppermute | solution.py:17
  91.7 14.6 %collective-permute-start.5 = (bf16[1,36,3584]{2,1,0:T(8,128)(2,1)}, bf16[1,36,3584]{2,1,0:T(8,128)(2,1)S(1)}, u32[]{:S(2)}, u32[]{:S(2)}) collective-permute-start(bf16[1,36,3584]{2,1,0:T(8,128)(2,1)} %get-tuple-element.31), channel_id=1, source_target_pairs={{0,20},{2,22},{4,24},{6,26},{8,28},{10,30},{12,0},{14,2},{16,4},{1... | collective-permute-start | bytes 774152 | tf_op jit(solution)/shard_map/ppermute | solution.py:17
  106.3 9.5 %collective-permute-start.6 = (bf16[1,36,3584]{2,1,0:T(8,128)(2,1)}, bf16[1,36,3584]{2,1,0:T(8,128)(2,1)S(1)}, u32[]{:S(2)}, u32[]{:S(2)}) collective-permute-start(bf16[1,36,3584]{2,1,0:T(8,128)(2,1)} %get-tuple-element.30), channel_id=1, source_target_pairs={{0,18},{2,20},{4,22},{6,24},{8,26},{10,28},{12,30},{14,0},{16,2},{... | collective-permute-start | bytes 774152 | tf_op jit(solution)/shard_map/ppermute | solution.py:17
  115.8 33.1 %collective-permute-start.7 = (bf16[1,36,3584]{2,1,0:T(8,128)(2,1)S(1)}, bf16[1,36,3584]{2,1,0:T(8,128)(2,1)S(1)}, u32[]{:S(2)}, u32[]{:S(2)}) collective-permute-start(bf16[1,36,3584]{2,1,0:T(8,128)(2,1)S(1)} %get-tuple-element.29), channel_id=1, source_target_pairs={{0,16},{2,18},{4,20},{6,22},{8,24},{10,26},{12,28},{14,30},{16,0},... | collective-permute-start | bytes 774152 | tf_op jit(solution)/shard_map/ppermute | solution.py:17
  148.8 13.5 %collective-permute-start.8 = (bf16[1,36,3584]{2,1,0:T(8,128)(2,1)}, bf16[1,36,3584]{2,1,0:T(8,128)(2,1)S(1)}, u32[]{:S(2)}, u32[]{:S(2)}) collective-permute-start(bf16[1,36,3584]{2,1,0:T(8,128)(2,1)} %get-tuple-element.28), channel_id=1, source_target_pairs={{0,14},{2,16},{4,18},{6,20},{8,22},{10,24},{12,26},{14,28},{16,30}... | collective-permute-start | bytes 774152 | tf_op jit(solution)/shard_map/ppermute | solution.py:17
  162.3 7.5 %collective-permute-start.9 = (bf16[1,36,3584]{2,1,0:T(8,128)(2,1)S(1)}, bf16[1,36,3584]{2,1,0:T(8,128)(2,1)S(1)}, u32[]{:S(2)}, u32[]{:S(2)}) collective-permute-start(bf16[1,36,3584]{2,1,0:T(8,128)(2,1)S(1)} %copy-done.6), channel_id=1, source_target_pairs={{0,12},{2,14},{4,16},{6,18},{8,20},{10,22},{12,24},{14,26},{16,28}... | collective-permute-start | bytes 774152 | tf_op jit(solution)/shard_map/ppermute | solution.py:17
  169.9 12.6 %collective-permute-start.10 = (bf16[1,36,3584]{2,1,0:T(8,128)(2,1)S(1)}, bf16[1,36,3584]{2,1,0:T(8,128)(2,1)S(1)}, u32[]{:S(2)}, u32[]{:S(2)}) collective-permute-start(bf16[1,36,3584]{2,1,0:T(8,128)(2,1)S(1)} %copy-done.5), channel_id=1, source_target_pairs={{0,10},{2,12},{4,14},{6,16},{8,18},{10,20},{12,22},{14,24},{16,26}... | collective-permute-start | bytes 774152 | tf_op jit(solution)/shard_map/ppermute | solution.py:17
  188.7 163.6 %all-gather.7.cloned.1.call-start = ((), (), s32[]{:S(2)}) async-start(), calls=%async_computation.8 | async-start | bytes 12386304 | tf_op jit(solution)/shard_map/all_gather | solution.py:82
  304.2 100.4 %reduce-scatter.3.cloned.1.call-start = ((), (), s32[]{:S(2)}) async-start(), calls=%async_computation.5 | async-start | bytes 27525120 | tf_op jit(solution)/shard_map/reduce_scatter | solution.py:90
  352.0 80.8 %reduce-scatter.5.cloned.1.call-start = ((), (), s32[]{:S(2)}) async-start(), calls=%async_computation.6 | async-start | bytes 27525120 | tf_op jit(solution)/shard_map/reduce_scatter | solution.py:91
  410.8 107.5 %all-to-all-start = ((bf16[16,36,3584]{2,1,0:T(8,128)(2,1)}), bf16[16,36,3584]{2,1,0:T(8,128)(2,1)}, u32[]{:S(2)}, u32[]{:S(2)}) async-start(bf16[16,36,3584]{2,1,0:T(8,128)(2,1)} %convert_bitcast_fusion.1), calls=%async_computation.1 | async-start | bytes 9175040 | tf_op jit(solution)/shard_map/all_to_all | solution.py:94
  439.0 84.4 %copy-start.9 = (s32[64,8]{0,1:T(8,128)S(1)}, s32[64,8]{0,1:T(8,128)}, u32[]{:S(2)}) copy-start(s32[64,8]{0,1:T(8,128)} %param.9) | copy-start | bytes 6148
  439.0 84.6 %copy-start.8 = (s32[512]{0:T(512)S(1)}, s32[512]{0:T(512)}, u32[]{:S(2)}) copy-start(s32[512]{0:T(512)} %copy-done.7) | copy-start | bytes 6148
  518.3 106.4 %all-to-all-start.2 = ((bf16[16,36,3584]{2,1,0:T(8,128)(2,1)}), bf16[16,36,3584]{2,1,0:T(8,128)(2,1)}, u32[]{:S(2)}, u32[]{:S(2)}) async-start(bf16[16,36,3584]{2,1,0:T(8,128)(2,1)} %convert_bitcast_fusion), calls=%async_computation.4 | async-start | bytes 9175040 | tf_op jit(solution)/shard_map/all_to_all | solution.py:97
  523.7 9.9 %copy-start.4 = (bf16[1152,512]{1,0:T(8,128)(2,1)S(1)}, bf16[1152,512]{1,0:T(8,128)(2,1)}, u32[]{:S(2)}) copy-start(bf16[1152,512]{1,0:T(8,128)(2,1)} %fusion.17) | copy-start | bytes 3538948
  631.7 16.2 %copy-start.1 = (bf16[64,3584]{1,0:T(8,128)(2,1)S(1)}, bf16[64,3584]{1,0:T(8,128)(2,1)}, u32[]{:S(2)}) copy-start(bf16[64,3584]{1,0:T(8,128)(2,1)} %param.8) | copy-start | bytes 1376260
Sparse Core Ops, SparseCore 0:
  188.8 21.7 all-gather.4
  304.3 20.0 all-gather.6
  352.1 28.2 reduce-scatter.2
  404.6 28.1 reduce-scatter.4
